TPU v7x, 32 devices: a whole 2x2x4 slice. The times are simulated.
32 devices in a mesh: seq: 2 (over core), ctx: 4 (over z), fsdp: 4 (over y, x).
Axes of the slice: x: 2, y: 2, z: 4, core: 2. Of those that a mesh axis runs over, the one named last changes fastest.
Arguments:
- inputs: bfloat16 [8, 1024, 640], P(('seq', 'fsdp'), 'ctx'), may hold values from -6 to 6
- positions: int32 [8, 1024], P(('seq', 'fsdp'), 'ctx'), may hold values from 0 to 1023, as said below
- block_ids: int32 [8, 8], P(('seq', 'fsdp'), 'ctx'), may hold values from 0 to 7, as said below
- w_query: bfloat16 [640, 1024], P('fsdp'), may hold values from -0.25 to 0.25
- w_key: bfloat16 [640, 256], P('fsdp'), may hold values from -0.25 to 0.25
- w_value: bfloat16 [640, 256], P('fsdp'), may hold values from -0.25 to 0.25
- w_out: bfloat16 [1024, 640], P('fsdp'), may hold values from -0.1875 to 0.1875
- w_gate: bfloat16 [640, 2048], P(None, 'fsdp'), may hold values from -0.25 to 0.25
- w_up: bfloat16 [640, 2048], P(None, 'fsdp'), may hold values from -0.25 to 0.25
- w_down: bfloat16 [2048, 640], P('fsdp'), may hold values from -0.125 to 0.125
- gain_in: bfloat16 [640], P('fsdp'), may hold values from 0.25 to 1.75
- gain_query: bfloat16 [256], P('fsdp'), may hold values from 0.25 to 1.75
- gain_key: bfloat16 [256], P('fsdp'), may hold values from 0.25 to 1.75
- gain_attn: bfloat16 [640], P('fsdp'), may hold values from 0.25 to 1.75
- gain_pre: bfloat16 [640], P('fsdp'), may hold values from 0.25 to 1.75
- gain_post: bfloat16 [640], P('fsdp'), may hold values from 0.25 to 1.75
- cotangent: bfloat16 [8, 1024, 640], P(('seq', 'fsdp'), 'ctx'), may hold values from -6 to 6
Outputs:
- result: float32 [8, 1024, 640], P(('seq', 'fsdp'), 'ctx')
- input_grad: float32 [8, 1024, 640], P(('seq', 'fsdp'), 'ctx')
- grad_w_query: float32 [640, 1024], P('fsdp')
- grad_w_key: float32 [640, 256], P('fsdp')
- grad_w_value: float32 [640, 256], P('fsdp')
- grad_w_out: float32 [1024, 640], P('fsdp')
- grad_w_gate: float32 [640, 2048], P(None, 'fsdp')
- grad_w_up: float32 [640, 2048], P(None, 'fsdp')
- grad_w_down: float32 [2048, 640], P('fsdp')
- grad_gain_in: float32 [640], P('fsdp')
- grad_gain_query: float32 [256], P('fsdp')
- grad_gain_key: float32 [256], P('fsdp')
- grad_gain_attn: float32 [640], P('fsdp')
- grad_gain_pre: float32 [640], P('fsdp')
- grad_gain_post: float32 [640], P('fsdp')
Inputs may be any that keep to these rules, and one draw needn't show every extreme that they name: `block_ids`: in every sequence the entries at 2 c and 2 c + 1 are b and 7 - b with b below 4, so a sequence's entries are a permutation of its blocks. `positions`: A token's position counts the tokens before it in its document, documents following one another in the order given by order; every document has at most 1024 tokens and the first of each sequence exactly 1024.
All inputs are finite; a program needn't handle non-finite values.
Results may differ from a plain program's by a relative error of at most 0.022.
Values may be sent and summed in bfloat16 or wider, within the bound.
No kernel may reach another device: no remote copies, remote signals or barrier semaphores. Data moves between devices by JAX's collectives and lax.ppermute only.
A program may use at most 192 MiB of HBM per device.

v0:
```python
import jax
import jax.numpy as jnp
from jax import lax
from jax.sharding import PartitionSpec as P

EPS = 1e-06
THETA = 1000000.0
NEG = -1e30


def matmul(left, right):
    return jnp.dot(left, right, preferred_element_type=jnp.float32)


def inner_cols(left, right):
    return lax.dot_general(
        left, right, (((1,), (1,)), ((), ())), preferred_element_type=jnp.float32
    )


def inner_rows(left, right):
    return lax.dot_general(
        left, right, (((0,), (0,)), ((), ())), preferred_element_type=jnp.float32
    )


def norm_fwd(value, gain):
    inverse = lax.rsqrt(jnp.mean(value * value, axis=-1, keepdims=True) + EPS)
    return (value * inverse * gain, inverse)


def norm_back(value, inverse, gain, grad):
    scaled = value * inverse
    gain_grad = jnp.sum((grad * scaled).reshape(-1, value.shape[-1]), axis=0)
    weighted = grad * gain
    value_grad = inverse * (weighted - scaled * jnp.mean(weighted * scaled, axis=-1, keepdims=True))
    return (value_grad, gain_grad)


def rotate(value, cosine, sine_table):
    half = value.shape[-1] // 2
    first = value[..., :half]
    second = value[..., half:]
    return jnp.concatenate(
        [first * cosine - second * sine_table, second * cosine + first * sine_table], axis=-1
    )


def tables(positions, head_size):
    half = head_size // 2
    freq = 1.0 / THETA ** (jnp.arange(half, dtype=jnp.float32) * 2.0 / head_size)
    angle = positions.astype(jnp.float32)[:, None] * freq[None, :]
    return (jnp.cos(angle), jnp.sin(angle))


def gelu_tanh(value):
    return jax.nn.gelu(value, approximate=True)


def attend_forward(queries, key_rows, values, query_order, key_order, score_scale):
    allowed = key_order[None, :] <= query_order[:, None]
    outputs = []
    logsums = []
    for head_index in range(queries.shape[1]):
        scores = inner_cols(queries[:, head_index], key_rows) * score_scale
        scores = jnp.where(allowed, scores, NEG)
        highest = jnp.max(scores, axis=-1, keepdims=True)
        weights = jnp.exp(scores - highest)
        summed = jnp.sum(weights, axis=-1, keepdims=True)
        probs = (weights / summed).astype(jnp.bfloat16)
        outputs.append(matmul(probs, values))
        logsums.append(highest + jnp.log(summed))
    return (jnp.stack(outputs, axis=1), jnp.stack(logsums, axis=1))


def attend_backward(
    queries, key_rows, values, query_order, key_order, score_scale, logsums, out_grad
):
    allowed = key_order[None, :] <= query_order[:, None]
    query_grads = []
    key_grad = jnp.zeros(key_rows.shape, jnp.float32)
    value_grad = jnp.zeros(values.shape, jnp.float32)
    for head_index in range(queries.shape[1]):
        query_head = queries[:, head_index]
        grad_head = out_grad[:, head_index]
        scores = inner_cols(query_head, key_rows) * score_scale
        scores = jnp.where(allowed, scores, NEG)
        probs = jnp.exp(scores - logsums[:, head_index])
        value_grad = value_grad + inner_rows(probs.astype(jnp.bfloat16), grad_head)
        prob_grad = inner_cols(grad_head, values)
        weighted = jnp.sum(probs * prob_grad, axis=-1, keepdims=True)
        score_grad = (probs * (prob_grad - weighted)).astype(jnp.bfloat16)
        query_grads.append(matmul(score_grad, key_rows) * score_scale)
        key_grad = key_grad + inner_rows(score_grad, query_head) * score_scale
    return (jnp.stack(query_grads, axis=1), key_grad, value_grad)


def on_device(
    inputs,
    positions,
    block_ids,
    w_query,
    w_key,
    w_value,
    w_out,
    w_gate,
    w_up,
    w_down,
    gain_in,
    gain_query,
    gain_key,
    gain_attn,
    gain_pre,
    gain_post,
    cotangent,
):
    gathered = (
        lax.all_gather(w_query, "fsdp", axis=0, tiled=True),
        lax.all_gather(w_key, "fsdp", axis=0, tiled=True),
        lax.all_gather(w_value, "fsdp", axis=0, tiled=True),
        lax.all_gather(w_out, "fsdp", axis=0, tiled=True),
        lax.all_gather(gain_in, "fsdp", axis=0, tiled=True),
        lax.all_gather(gain_query, "fsdp", axis=0, tiled=True),
        lax.all_gather(gain_key, "fsdp", axis=0, tiled=True),
        lax.all_gather(gain_attn, "fsdp", axis=0, tiled=True),
        lax.all_gather(gain_pre, "fsdp", axis=0, tiled=True),
        lax.all_gather(gain_post, "fsdp", axis=0, tiled=True),
    )
    query_full, key_full, value_full, out_full = (
        gathered[0],
        gathered[1],
        gathered[2],
        gathered[3],
    )
    norm_in, norm_query, norm_key, norm_attn, norm_pre, norm_post = [
        member.astype(jnp.float32) for member in gathered[4:]
    ]
    seq_count, seq_rows, model_width = inputs.shape
    row_count = seq_count * seq_rows
    head_size = norm_query.shape[0]
    head_count = query_full.shape[1] // head_size
    half_rows = seq_rows // 2
    score_scale = head_size ** (-0.5)
    offsets = jnp.arange(half_rows, dtype=jnp.int32)
    query_order = (block_ids[:, :, None] * half_rows + offsets[None, None, :]).reshape(
        seq_count, seq_rows
    )
    cosine, sine_table = tables(positions.reshape(row_count), head_size)
    residual = inputs.astype(jnp.float32).reshape(row_count, model_width)
    normed_in, inverse_in = norm_fwd(residual, norm_in)
    hidden_in = normed_in.astype(jnp.bfloat16)
    query_pre = matmul(hidden_in, query_full).reshape(row_count, head_count, head_size)
    key_pre = matmul(hidden_in, key_full)
    value_pre = matmul(hidden_in, value_full)
    query_normed, inverse_query = norm_fwd(query_pre, norm_query)
    key_normed, inverse_key = norm_fwd(key_pre, norm_key)
    queries = rotate(query_normed, cosine[:, None], sine_table[:, None]).astype(jnp.bfloat16)
    key_rows = rotate(key_normed, cosine, sine_table).astype(jnp.bfloat16)
    values = value_pre.astype(jnp.bfloat16)
    key_all, value_all, block_all = (
        lax.all_gather(key_rows.reshape(seq_count, seq_rows, head_size), "ctx", axis=1, tiled=True),
        lax.all_gather(values.reshape(seq_count, seq_rows, head_size), "ctx", axis=1, tiled=True),
        lax.all_gather(block_ids.astype(jnp.bfloat16), "ctx", axis=1, tiled=True),
    )
    key_order = (
        block_all.astype(jnp.int32)[:, :, None] * half_rows + offsets[None, None, :]
    ).reshape(seq_count, -1)
    seq_index = 0
    seq_out, seq_logsum = attend_forward(
        queries,
        key_all[seq_index],
        value_all[seq_index],
        query_order[seq_index],
        key_order[seq_index],
        score_scale,
    )
    logsum_list = [seq_logsum]
    context = seq_out.astype(jnp.bfloat16).reshape(row_count, head_count * head_size)
    attn_out = matmul(context, out_full)
    attn_normed, inverse_attn = norm_fwd(attn_out, norm_attn)
    middle = residual + attn_normed
    pre_normed, inverse_pre = norm_fwd(middle, norm_pre)
    ffn_in = pre_normed.astype(jnp.bfloat16)
    gate_full, up_full, down_full = (w_gate, w_up, w_down)
    ffn_rows = lax.all_gather(
        ffn_in.reshape(seq_count, seq_rows, model_width), "fsdp", axis=0, tiled=True
    ).reshape(-1, model_width)
    gate_pre = matmul(ffn_rows, gate_full)
    up_pre = matmul(ffn_rows, up_full)
    activated, gelu_pull = jax.vjp(gelu_tanh, gate_pre)
    mixed = (activated * up_pre).astype(jnp.bfloat16)
    down_part = matmul(mixed, down_full)
    ffn_out = (
        lax.psum_scatter(
            down_part.reshape(-1, seq_rows, model_width).astype(jnp.bfloat16),
            "fsdp",
            scatter_dimension=0,
            tiled=True,
        )
        .astype(jnp.float32)
        .reshape(row_count, model_width)
    )
    ffn_normed, inverse_post = norm_fwd(ffn_out, norm_post)
    result = middle + ffn_normed
    grad_output = cotangent.astype(jnp.float32).reshape(row_count, model_width)
    ffn_grad, grad_post = norm_back(ffn_out, inverse_post, norm_post, grad_output)
    ffn_grad = ffn_grad.astype(jnp.bfloat16)
    ffn_grad_rows = lax.all_gather(
        ffn_grad.reshape(seq_count, seq_rows, model_width), "fsdp", axis=0, tiled=True
    ).reshape(-1, model_width)
    mixed_grad = inner_cols(ffn_grad_rows, down_full)
    grad_down = inner_rows(mixed, ffn_grad_rows)
    gate_grad = gelu_pull(mixed_grad * up_pre)[0].astype(jnp.bfloat16)
    up_grad = (mixed_grad * activated).astype(jnp.bfloat16)
    grad_gate = inner_rows(ffn_rows, gate_grad)
    grad_up = inner_rows(ffn_rows, up_grad)
    pre_part = inner_cols(gate_grad, gate_full) + inner_cols(up_grad, up_full)
    pre_grad = (
        lax.psum_scatter(
            pre_part.reshape(-1, seq_rows, model_width).astype(jnp.bfloat16),
            "fsdp",
            scatter_dimension=0,
            tiled=True,
        )
        .astype(jnp.float32)
        .reshape(row_count, model_width)
    )
    middle_part, grad_pre = norm_back(middle, inverse_pre, norm_pre, pre_grad)
    middle_grad = grad_output + middle_part
    attn_grad, grad_attn_gain = norm_back(attn_out, inverse_attn, norm_attn, middle_grad)
    attn_grad = attn_grad.astype(jnp.bfloat16)
    grad_out_w = inner_rows(context, attn_grad)
    context_grad = (
        inner_cols(attn_grad, out_full)
        .astype(jnp.bfloat16)
        .reshape(row_count, head_count, head_size)
    )
    seq_index = 0
    seq_query_grad, seq_key_grad, seq_value_grad = attend_backward(
        queries,
        key_all[seq_index],
        value_all[seq_index],
        query_order[seq_index],
        key_order[seq_index],
        score_scale,
        logsum_list[seq_index],
        context_grad,
    )
    key_back_list = [seq_key_grad]
    value_back_list = [seq_value_grad]
    key_grad_all = jnp.stack(key_back_list, axis=0)
    value_grad_all = jnp.stack(value_back_list, axis=0)
    key_back, value_back = (
        lax.psum_scatter(
            key_grad_all.astype(jnp.bfloat16), "ctx", scatter_dimension=1, tiled=True
        ).astype(jnp.float32),
        lax.psum_scatter(
            value_grad_all.astype(jnp.bfloat16), "ctx", scatter_dimension=1, tiled=True
        ).astype(jnp.float32),
    )
    key_back = key_back.reshape(row_count, head_size)
    value_back = value_back.reshape(row_count, head_size).astype(jnp.bfloat16)
    key_normed_grad = rotate(key_back, cosine, -sine_table)
    key_pre_grad, grad_key_gain = norm_back(key_pre, inverse_key, norm_key, key_normed_grad)
    key_pre_grad = key_pre_grad.astype(jnp.bfloat16)
    query_normed_grad = rotate(seq_query_grad, cosine[:, None], -sine_table[:, None])
    query_pre_grad, grad_query_gain = norm_back(
        query_pre, inverse_query, norm_query, query_normed_grad
    )
    query_pre_grad = query_pre_grad.astype(jnp.bfloat16).reshape(row_count, head_count * head_size)
    hidden_grad = (
        inner_cols(query_pre_grad, query_full)
        + inner_cols(key_pre_grad, key_full)
        + inner_cols(value_back, value_full)
    )
    input_part, grad_in_gain = norm_back(residual, inverse_in, norm_in, hidden_grad)
    input_grad = middle_grad + input_part
    grad_query_w = inner_rows(hidden_in, query_pre_grad)
    grad_key_w = inner_rows(hidden_in, key_pre_grad)
    grad_value_w = inner_rows(hidden_in, value_back)
    attn_shards = (
        lax.psum_scatter(
            grad_query_w.astype(jnp.bfloat16), "fsdp", scatter_dimension=0, tiled=True
        ).astype(jnp.float32),
        lax.psum_scatter(
            grad_key_w.astype(jnp.bfloat16), "fsdp", scatter_dimension=0, tiled=True
        ).astype(jnp.float32),
        lax.psum_scatter(
            grad_value_w.astype(jnp.bfloat16), "fsdp", scatter_dimension=0, tiled=True
        ).astype(jnp.float32),
        lax.psum_scatter(
            grad_out_w.astype(jnp.bfloat16), "fsdp", scatter_dimension=0, tiled=True
        ).astype(jnp.float32),
        lax.psum_scatter(
            grad_in_gain.astype(jnp.bfloat16), "fsdp", scatter_dimension=0, tiled=True
        ).astype(jnp.float32),
        lax.psum_scatter(
            grad_query_gain.astype(jnp.bfloat16), "fsdp", scatter_dimension=0, tiled=True
        ).astype(jnp.float32),
        lax.psum_scatter(
            grad_key_gain.astype(jnp.bfloat16), "fsdp", scatter_dimension=0, tiled=True
        ).astype(jnp.float32),
        lax.psum_scatter(
            grad_attn_gain.astype(jnp.bfloat16), "fsdp", scatter_dimension=0, tiled=True
        ).astype(jnp.float32),
        lax.psum_scatter(
            grad_pre.astype(jnp.bfloat16), "fsdp", scatter_dimension=0, tiled=True
        ).astype(jnp.float32),
        lax.psum_scatter(
            grad_post.astype(jnp.bfloat16), "fsdp", scatter_dimension=0, tiled=True
        ).astype(jnp.float32),
    )
    ordered = tuple(attn_shards) + (grad_gate, grad_up, grad_down)
    totals = lax.psum(
        (
            ordered[0],
            ordered[1],
            ordered[2],
            ordered[3],
            ordered[4],
            ordered[5],
            ordered[6],
            ordered[7],
            ordered[8],
            ordered[9],
            ordered[10],
            ordered[11],
            ordered[12],
        ),
        ("seq", "ctx"),
    )
    result = result.reshape(seq_count, seq_rows, model_width)
    input_grad = input_grad.reshape(seq_count, seq_rows, model_width)
    return (
        result,
        input_grad,
        totals[0],
        totals[1],
        totals[2],
        totals[3],
        totals[10],
        totals[11],
        totals[12],
        totals[4],
        totals[5],
        totals[6],
        totals[7],
        totals[8],
        totals[9],
    )


def solution(mesh):
    in_specs = (
        P(("seq", "fsdp"), "ctx", None),
        P(("seq", "fsdp"), "ctx"),
        P(("seq", "fsdp"), "ctx"),
        P("fsdp", None),
        P("fsdp", None),
        P("fsdp", None),
        P("fsdp", None),
        P(None, "fsdp"),
        P(None, "fsdp"),
        P("fsdp", None),
        P("fsdp"),
        P("fsdp"),
        P("fsdp"),
        P("fsdp"),
        P("fsdp"),
        P("fsdp"),
        P(("seq", "fsdp"), "ctx", None),
    )
    out_specs = (
        P(("seq", "fsdp"), "ctx", None),
        P(("seq", "fsdp"), "ctx", None),
        P("fsdp", None),
        P("fsdp", None),
        P("fsdp", None),
        P("fsdp", None),
        P(None, "fsdp"),
        P(None, "fsdp"),
        P("fsdp", None),
        P("fsdp"),
        P("fsdp"),
        P("fsdp"),
        P("fsdp"),
        P("fsdp"),
        P("fsdp"),
    )
    return jax.shard_map(
        on_device, mesh=mesh, in_specs=in_specs, out_specs=out_specs, check_vma=False
    )
```

profile of v0, /device:TPU:0, one launch (start us, length us, event | category | flops | bytes accessed | tf_op | source)
XLA Modules:
  0.0 594.1 jit_solution(3232758856841202865)
XLA Ops:
  10.0 1.3 fusion.134
  16.1 13.4 %all-reduce = bf16[8]{0:T(256)(128)(2,1)S(1)} all-reduce(bf16[8]{0:T(256)(128)(2,1)S(1)} %dynamic-update-slice), channel_id=1, replica_groups=mesh['seq'=2,'ctx'=4,'fsdp'=4] {'ctx'}, use_global_device_ids=true, to_apply=%add | all-reduce | flops 8 | bytes 32
  34.7 10.8 %all-reduce.18 = (bf16[640]{0:T(1024)(128)(2,1)S(1)}, bf16[256]{0:T(256)(128)(2,1)S(1)}, bf16[256]{0:T(256)(128)(2,1)S(1)}, bf16[640]{0:T(1024)(128)(2,1)S(1)}, ...) all-reduce(bf16[640]{0:T(1024)(128)(2,1)S(1)} %dynamic-update-slice, ...), channel_id=1, replica_groups=mesh['seq'=2,'ctx'=4,'fsdp'=4] {'fsdp'}, use_global_device_ids=true, to_apply=%add.1 | all-reduce | flops 3072 | bytes 12288
  45.6 9.6 %all_gather.49 = bf16[640,256]{1,0:T(8,128)(2,1)S(1)} all-gather(bf16[160,256]{1,0:T(8,128)(2,1)} %param.21), channel_id=1, replica_groups=mesh['seq'=2,'ctx'=4,'fsdp'=4] {'fsdp'}, dimensions={0}, use_global_device_ids=true | all-gather | bytes 409600 | tf_op jit(solution)/shard_map/all_gather | solution.py:119
  55.2 1.5 multiply_reduce_fusion.13
  56.8 11.6 %all_gather.52 = bf16[640,256]{1,0:T(8,128)(2,1)S(1)} all-gather(bf16[160,256]{1,0:T(8,128)(2,1)S(1)} %copy-done.58), channel_id=1, replica_groups=mesh['seq'=2,'ctx'=4,'fsdp'=4] {'fsdp'}, dimensions={0}, use_global_device_ids=true | all-gather | bytes 409600 | tf_op jit(solution)/shard_map/all_gather | solution.py:120
  68.7 15.6 %all-gather = bf16[1024,256]{1,0:T(8,128)(2,1)} all-gather(bf16[256,256]{1,0:T(8,128)(2,1)S(1)} %convolution_convert_fusion.10), channel_id=2, replica_groups=mesh['seq'=2,'ctx'=4,'fsdp'=4] {'ctx'}, dimensions={0}, use_global_device_ids=true | all-gather | bytes 655360 | tf_op jit(solution)/shard_map/all_gather | solution.py:162
  85.7 14.7 %all_gather.51 = bf16[1,1024,256]{1,2,0:T(8,128)(2,1)S(1)} all-gather(bf16[1,256,256]{1,2,0:T(8,128)(2,1)S(1)} %pad_maximum_fusion.5), channel_id=1, replica_groups=mesh['seq'=2,'ctx'=4,'fsdp'=4] {'ctx'}, dimensions={1}, use_global_device_ids=true | all-gather | bytes 655360 | tf_op jit(solution)/shard_map/all_gather | solution.py:161
  100.4 2.4 copy.46
  102.8 2.0 multiply_reduce_fusion.6
  112.1 2.2 multiply_reduce_fusion.10
  117.1 27.0 %all-gather.13.cloned.1.call-done = bf16[1024,640]{1,0:T(8,128)(2,1)} async-done(((bf16[256,640]{1,0:T(8,128)(2,1)}), bf16[1024,640]{1,0:T(8,128)(2,1)}) %all-gather.13.cloned.1.call-update) | async-done | bytes 1310736 | tf_op jit(solution)/shard_map/all_gather | solution.py:185
  144.1 2.6 fusion.139
  146.7 2.6 multiply_convert_fusion.1
  150.3 2.0 convolution_convert_fusion.2
  153.7 28.2 %reduce-scatter.25.cloned.1.call-done = bf16[1,256,640]{2,1,0:T(8,128)(2,1)} async-done(((bf16[4,256,640]{2,1,0:T(8,128)(2,1)}), bf16[1,256,640]{2,1,0:T(8,128)(2,1)}) %reduce-scatter.25.cloned.1.call-update) | async-done | bytes 327696
  183.0 2.0 fusion.65
  185.0 2.0 fusion.64
  187.1 28.9 %all-gather.11.cloned.1.call-done = bf16[4,256,640]{2,1,0:T(8,128)(2,1)} async-done(((bf16[1,256,640]{2,1,0:T(8,128)(2,1)}), bf16[4,256,640]{2,1,0:T(8,128)(2,1)}) %all-gather.11.cloned.1.call-update) | async-done | bytes 1310736 | tf_op jit(solution)/shard_map/all_gather | solution.py:208
  216.0 5.0 multiply_convert_fusion
  222.6 2.1 add_convert_fusion
  230.0 24.2 %reduce-scatter.27.cloned.1.call-done = bf16[1,256,640]{2,1,0:T(8,128)(2,1)} async-done(((bf16[4,256,640]{2,1,0:T(8,128)(2,1)}), bf16[1,256,640]{2,1,0:T(8,128)(2,1)}) %reduce-scatter.27.cloned.1.call-update) | async-done | bytes 327696
  254.2 2.1 fusion.66
  256.3 3.5 multiply_reduce_fusion.7
  263.2 2.8 fusion.133
  266.4 1.3 multiply_reduce_fusion.5
  267.8 1.3 multiply_reduce_fusion.4
  270.3 1.4 multiply_reduce_fusion.3
  273.7 2.0 multiply_convert_fusion.6
  281.9 13.5 %reduce-scatter.15.cloned.1.call-done = bf16[1,256,256]{2,1,0:T(8,128)(2,1)} async-done(((bf16[1,1024,256]{2,1,0:T(8,128)(2,1)}), bf16[1,256,256]{2,1,0:T(8,128)(2,1)}) %reduce-scatter.15.cloned.1.call-update) | async-done | bytes 131088 | tf_op jit(solution)/shard_map/reduce_scatter | solution.py:257
  295.5 2.0 convolution_convert_fusion.4
  297.6 20.7 %reduce-scatter.13.cloned.1.call-done = bf16[1,256,256]{1,2,0:T(8,128)(2,1)} async-done(((bf16[1,1024,256]{1,2,0:T(8,128)(2,1)}), bf16[1,256,256]{1,2,0:T(8,128)(2,1)}) %reduce-scatter.13.cloned.1.call-update) | async-done | bytes 131088 | tf_op jit(solution)/shard_map/reduce_scatter | solution.py:254
  321.3 1.6 convolution_convert_fusion
  323.7 1.4 fusion.14
  325.1 1.4 fusion.15
  328.1 1.7 convolution_convert_fusion.1
  331.3 3.5 fusion.144
  334.8 1.9 fusion.143
  336.7 1.9 fusion.142
  340.3 1.6 fusion.53
  341.9 10.0 %all-reduce.17 = (bf16[640]{0:T(1024)(128)(2,1)S(1)}, bf16[256]{0:T(256)(128)(2,1)S(1)}, bf16[256]{0:T(256)(128)(2,1)S(1)}, bf16[640]{0:T(1024)(128)(2,1)S(1)}, ...) all-reduce(bf16[640]{0:T(1024)(128)(2,1)S(1)} %get-tuple-element.21, ...), channel_id=12, replica_groups=mesh['seq'=2,'ctx'=4,'fsdp'=4] {'fsdp'}, use_global_device_ids=true, to_apply=%region_40.41.clone | all-reduce | flops 3072 | bytes 12288
  352.1 2.1 fusion.52
  354.3 16.3 %reduce-scatter.19.cloned.1.call-done = bf16[160,256]{1,0:T(8,128)(2,1)} async-done(((bf16[640,256]{1,0:T(8,128)(2,1)}), bf16[160,256]{1,0:T(8,128)(2,1)}) %reduce-scatter.19.cloned.1.call-update) | async-done | bytes 81936 | tf_op jit(solution)/shard_map/reduce_scatter | solution.py:285
  370.6 32.9 %reduce-scatter.23.cloned.1.call-done = bf16[256,640]{1,0:T(8,128)(2,1)} async-done(((bf16[1024,640]{1,0:T(8,128)(2,1)}), bf16[256,640]{1,0:T(8,128)(2,1)}) %reduce-scatter.23.cloned.1.call-update) | async-done | bytes 327696 | tf_op jit(solution)/shard_map/reduce_scatter | solution.py:291
  403.4 32.7 %reduce-scatter.17.cloned.1.call-done = bf16[160,1024]{1,0:T(8,128)(2,1)} async-done(((bf16[640,1024]{1,0:T(8,128)(2,1)}), bf16[160,1024]{1,0:T(8,128)(2,1)}) %reduce-scatter.17.cloned.1.call-update) | async-done | bytes 327696 | tf_op jit(solution)/shard_map/reduce_scatter | solution.py:282
  436.1 126.0 %all-reduce.23 = (f32[160,1024]{1,0:T(8,128)}, f32[160,256]{1,0:T(8,128)}, f32[160,256]{1,0:T(8,128)}, f32[256,640]{1,0:T(8,128)}, f32[160]{0:T(256)}, /*index=5...) all-reduce(bf16[160,1024]{1,0:T(8,128)(2,1)} %reduce-scatter.17.clo, ...), channel_id=1, replica_groups=mesh['seq'=2,'ctx'=4,'fsdp'=4] {'seq','ctx'}, use_global_device_ids=true, to_apply=%region_29.30 | all-reduce | flops 410368 | bytes 2463744 | tf_op jit(solution)/shard_map/psum | solution.py:314
  562.1 20.6 %all-reduce.22.cloned.1.call-done = (f32[640,512]{1,0:T(8,128)}, f32[640,512]{1,0:T(8,128)}, f32[512,640]{1,0:T(8,128)}) async-done(((f32[640,512]{1,0:T(8,128)}, f32[640,512]{1,0:T(8,128)}, f32[512,640]{1,0:T(8,128)}), (f32[640,512]{1,0:T(8,128)}, f32[640,512]{1,0:T(8,128)}, f32[512,640]{1,0:T(8,128)})) %all-reduce.22.cloned.1.call-update) | async-done | bytes 3932176 | tf_op jit(solution)/shard_map/psum | solution.py:314
  582.8 2.6 copy.107
  (330 shorter events, 54.8 us)
Async XLA Ops:
  7.2 143.1 %copy-start = (bf16[512,640]{1,0:T(8,128)(2,1)S(1)}, bf16[512,640]{1,0:T(8,128)(2,1)}, u32[]{:S(2)}) copy-start(bf16[512,640]{1,0:T(8,128)(2,1)} %param.26) | copy-start | bytes 1966084
  7.2 61.2 %copy-start.12 = (bf16[1,256,640]{2,1,0:T(8,128)(2,1)S(1)}, bf16[1,256,640]{2,1,0:T(8,128)(2,1)}, u32[]{:S(2)}) copy-start(bf16[1,256,640]{2,1,0:T(8,128)(2,1)} %param.17) | copy-start | bytes 983044
  7.2 49.6 %copy-start.58 = (bf16[160,256]{1,0:T(8,128)(2,1)S(1)}, bf16[160,256]{1,0:T(8,128)(2,1)}, u32[]{:S(2)}) copy-start(bf16[160,256]{1,0:T(8,128)(2,1)} %param.22) | copy-start | bytes 245764
  7.2 93.2 %all-gather.7.cloned.1.call-start = ((), (), s32[]{:S(2)}) async-start(), calls=%async_computation.8 | async-start | bytes 1638400 | tf_op jit(solution)/shard_map/all_gather | solution.py:118
  8.0 104.2 %all-gather.9.cloned.1.call-start = ((), (), s32[]{:S(2)}) async-start(), calls=%async_computation.9 | async-start | bytes 1638400 | tf_op jit(solution)/shard_map/all_gather | solution.py:121
  8.7 135.4 %all-gather.13.cloned.1.call-start = ((), (), s32[]{:S(2)}) async-start(), calls=%async_computation.17 | async-start | bytes 1638400 | tf_op jit(solution)/shard_map/all_gather | solution.py:185
  8.8 75.7 %copy-start.90 = (f32[128]{0:T(128)}, f32[128]{0:T(128)S(1)}, u32[]{:S(2)}) copy-start(f32[128]{0:T(128)S(1)} %negate_power_fusion) | copy-start | bytes 1540
  13.8 89.0 %copy-start.59 = (f32[256]{0:T(256)}, f32[256]{0:T(256)S(1)}, u32[]{:S(2)}) copy-start(f32[256]{0:T(256)S(1)} %add_rsqrt_fusion.5) | copy-start | bytes 3076
  16.1 69.6 %copy-start.75 = (f32[1,256]{1,0:T(1,128)}, f32[1,256]{1,0:T(1,128)S(1)}, u32[]{:S(2)}) copy-start(f32[1,256]{1,0:T(1,128)S(1)} %convert_element_type.233) | copy-start | bytes 3076
  29.7 76.0 %copy-start.92 = (s32[256]{0:T(256)}, s32[256]{0:T(256)S(1)}, u32[]{:S(2)}) copy-start(s32[256]{0:T(256)S(1)} %bitcast_add_fusion.1) | copy-start | bytes 3076
  45.5 59.4 %copy-start.71 = (f32[256]{0:T(256)}, f32[256]{0:T(256)S(1)}, u32[]{:S(2)}) copy-start(f32[256]{0:T(256)S(1)} %convert_element_type.232) | copy-start | bytes 3076
  45.5 38.9 %copy-start.73 = (f32[256]{0:T(256)}, f32[256]{0:T(256)S(1)}, u32[]{:S(2)}) copy-start(f32[256]{0:T(256)S(1)} %convert_element_type.236) | copy-start | bytes 3076
  45.6 60.1 %copy-start.80 = (s32[1024]{0:T(1024)}, s32[1024]{0:T(1024)S(1)}, u32[]{:S(2)}) copy-start(s32[1024]{0:T(1024)S(1)} %bitcast_add_fusion) | copy-start | bytes 12292
  55.2 30.4 %copy-start.39 = (bf16[640,256]{1,0:T(8,128)(2,1)}, bf16[640,256]{1,0:T(8,128)(2,1)S(1)}, u32[]{:S(2)}) copy-start(bf16[640,256]{1,0:T(8,128)(2,1)S(1)} %all_gather.49) | copy-start | bytes 983044
  56.8 28.9 %copy-start.35 = (f32[256,256]{0,1:T(8,128)}, f32[256,256]{0,1:T(8,128)S(1)}, u32[]{:S(2)}) copy-start(f32[256,256]{0,1:T(8,128)S(1)} %get-tuple-element.82) | copy-start | bytes 786436
  56.8 27.7 %copy-start.65 = (f32[256]{0:T(256)}, f32[256]{0:T(256)S(1)}, u32[]{:S(2)}) copy-start(f32[256]{0:T(256)S(1)} %add_rsqrt_fusion.4) | copy-start | bytes 3076
  68.4 17.3 %copy-start.41 = (bf16[640,256]{1,0:T(8,128)(2,1)}, bf16[640,256]{1,0:T(8,128)(2,1)S(1)}, u32[]{:S(2)}) copy-start(bf16[640,256]{1,0:T(8,128)(2,1)S(1)} %all_gather.52) | copy-start | bytes 983044
  85.7 19.4 %copy-start.43 = (f32[256,128]{0,1:T(8,128)}, f32[256,128]{0,1:T(8,128)S(1)}, u32[]{:S(2)}) copy-start(f32[256,128]{0,1:T(8,128)S(1)} %get-tuple-element.74) | copy-start | bytes 393220
  105.7 4.0 copy-start.5
  105.7 4.0 copy-start.82
  106.1 4.1 copy-start.2
  106.1 4.1 copy-start.83
  116.9 65.0 %reduce-scatter.25.cloned.1.call-start = ((), (), s32[]{:S(2)}) async-start(), calls=%async_computation.18 | async-start | bytes 1638400
  152.4 63.6 %all-gather.11.cloned.1.call-start = ((), (), s32[]{:S(2)}) async-start(), calls=%async_computation.10 | async-start | bytes 1638400 | tf_op jit(solution)/shard_map/all_gather | solution.py:208
  187.1 67.1 %reduce-scatter.27.cloned.1.call-start = ((), (), s32[]{:S(2)}) async-start(), calls=%async_computation.19 | async-start | bytes 1638400
  216.0 5.1 copy-start.51
  224.7 31.6 %copy-start.16 = (f32[256,640]{1,0:T(8,128)S(1)}, f32[256,640]{1,0:T(8,128)}, u32[]{:S(2)}) copy-start(f32[256,640]{1,0:T(8,128)} %copy-done.15) | copy-start | bytes 1966084
  224.7 70.7 %reduce-scatter.15.cloned.1.call-start = ((), (), s32[]{:S(2)}) async-start(), calls=%async_computation.12 | async-start | bytes 655360 | tf_op jit(solution)/shard_map/reduce_scatter | solution.py:257
  254.2 5.6 copy-start.68
  256.3 5.1 copy-start.23
  265.9 6.3 %copy-start.49 = (bf16[256,1,256]{2,1,0:T(2,128)(2,1)}, bf16[256,1,256]{2,1,0:T(2,128)(2,1)S(1)}, u32[]{:S(2)}) copy-start(bf16[256,1,256]{2,1,0:T(2,128)(2,1)S(1)} %get-tuple-element.62) | copy-start | bytes 393220
  273.7 44.6 %reduce-scatter.13.cloned.1.call-start = ((), (), s32[]{:S(2)}) async-start(), calls=%async_computation.11 | async-start | bytes 655360 | tf_op jit(solution)/shard_map/reduce_scatter | solution.py:254
  279.6 15.9 %copy-start.14 = (bf16[1,256,640]{2,1,0:T(8,128)(2,1)S(1)}, bf16[1,256,640]{2,1,0:T(8,128)(2,1)}, u32[]{:S(2)}) copy-start(bf16[1,256,640]{2,1,0:T(8,128)(2,1)} %param.17) | copy-start | bytes 983044
  279.6 15.9 %copy-start.60 = (f32[256]{0:T(256)S(1)}, f32[256]{0:T(256)}, u32[]{:S(2)}) copy-start(f32[256]{0:T(256)} %copy-done.59) | copy-start | bytes 3076
  280.7 38.5 %copy-start.76 = (f32[1,256]{1,0:T(1,128)S(1)}, f32[1,256]{1,0:T(1,128)}, u32[]{:S(2)}) copy-start(f32[1,256]{1,0:T(1,128)} %copy-done.75) | copy-start | bytes 3076
  280.7 38.5 %copy-start.91 = (f32[128]{0:T(128)S(1)}, f32[128]{0:T(128)}, u32[]{:S(2)}) copy-start(f32[128]{0:T(128)} %copy-done.90) | copy-start | bytes 1540
  280.7 39.1 %copy-start.36 = (f32[256,256]{0,1:T(8,128)S(1)}, f32[256,256]{0,1:T(8,128)}, u32[]{:S(2)}) copy-start(f32[256,256]{0,1:T(8,128)} %copy-done.35) | copy-start | bytes 786436
  280.7 39.1 %copy-start.66 = (f32[256]{0:T(256)S(1)}, f32[256]{0:T(256)}, u32[]{:S(2)}) copy-start(f32[256]{0:T(256)} %copy-done.65) | copy-start | bytes 3076
  280.7 39.1 %copy-start.74 = (f32[256]{0:T(256)S(1)}, f32[256]{0:T(256)}, u32[]{:S(2)}) copy-start(f32[256]{0:T(256)} %copy-done.73) | copy-start | bytes 3076
  281.9 39.4 %copy-start.26 = (bf16[256,4,256]{0,2,1:T(8,128)(2,1)S(1)}, bf16[256,4,256]{0,2,1:T(8,128)(2,1)}, u32[]{:S(2)}) copy-start(bf16[256,4,256]{0,2,1:T(8,128)(2,1)} %pad_maximum_fusion.2) | copy-start | bytes 1572868
  281.9 39.4 %copy-start.34 = (bf16[256,640]{1,0:T(8,128)(2,1)S(1)}, bf16[256,640]{1,0:T(8,128)(2,1)}, u32[]{:S(2)}) copy-start(bf16[256,640]{1,0:T(8,128)(2,1)} %copy-done.33) | copy-start | bytes 983044
  281.9 72.4 %reduce-scatter.21.cloned.1.call-start = ((), (), s32[]{:S(2)}) async-start(), calls=%async_computation.15 | async-start | bytes 409600 | tf_op jit(solution)/shard_map/reduce_scatter | solution.py:288
  297.5 73.0 %reduce-scatter.19.cloned.1.call-start = ((), (), s32[]{:S(2)}) async-start(), calls=%async_computation.14 | async-start | bytes 409600 | tf_op jit(solution)/shard_map/reduce_scatter | solution.py:285
  321.2 82.2 %reduce-scatter.23.cloned.1.call-start = ((), (), s32[]{:S(2)}) async-start(), calls=%async_computation.16 | async-start | bytes 1638400 | tf_op jit(solution)/shard_map/reduce_scatter | solution.py:291
  323.0 113.1 %reduce-scatter.17.cloned.1.call-start = ((), (), s32[]{:S(2)}) async-start(), calls=%async_computation.13 | async-start | bytes 1638400 | tf_op jit(solution)/shard_map/reduce_scatter | solution.py:282
  329.9 252.9 %all-reduce.22.cloned.1.call-start = ((), (), s32[]{:S(2)}) async-start(), calls=%async_computation.20 | async-start | bytes 7864320 | tf_op jit(solution)/shard_map/psum | solution.py:314
  340.3 11.9 %copy-start.21 = (f32[256,640]{1,0:T(8,128)S(1)}, f32[256,640]{1,0:T(8,128)}, u32[]{:S(2)}) copy-start(f32[256,640]{1,0:T(8,128)} %copy-done.20) | copy-start | bytes 1966084
  582.8 4.7 copy-start.1
  (64 other events, 115.2 us)
Sparse Core Ops, SparseCore 0:
  9.9 32.2 all-gather.6
  44.0 29.9 all-gather.8
  117.0 27.0 all-gather.12
  152.5 29.3 reduce-scatter.24
  187.2 28.7 all-gather.10
  224.9 29.2 reduce-scatter.26
  273.8 21.6 reduce-scatter.14
  298.3 19.9 reduce-scatter.12
  321.0 22.5 reduce-scatter.20
  346.2 24.2 reduce-scatter.18
  374.1 29.3 reduce-scatter.22
  406.8 29.2 reduce-scatter.16
  439.3 143.4 all-reduce.21
where the time goes:
time: 595 us; the launch traced here: 594 us
  waiting for transfers between devices  247 us (42%)
  blocking collectives  212 us (36%)
  matrix products  55 us (9%)
  other arithmetic  32.4 us (5%)
  local copies, waits for them, and re-layouts  28.7 us (5%)
  between operations  18.5 us (3%)
    psum x1, blocking collectives, on_device(): lax.psum((ordered[0], ordered[1], ordered[2], ordered[3], ordered[4], ord...  126 us
    unnamed x15, waiting for transfers between devices  53.9 us
    unnamed x3, blocking collectives  34.2 us
    reduce_scatter x1, waiting for transfers between devices, on_device(): lax.psum_scatter(grad_out_w.astype(jnp.bfloat16), 'fsdp', scatter_dimensi...  32.9 us
    reduce_scatter x1, waiting for transfers between devices, on_device(): lax.psum_scatter(grad_query_w.astype(jnp.bfloat16), 'fsdp', scatter_dimen...  32.7 us
    all_gather x1, waiting for transfers between devices, on_device(): lax.all_gather(ffn_grad.reshape(seq_count, seq_rows, model_width), 'fsdp'...  28.9 us
    all_gather x1, waiting for transfers between devices, on_device(): lax.all_gather(ffn_in.reshape(seq_count, seq_rows, model_width), 'fsdp',...  27 us
    unnamed x217, local copies, waits for them, and re-layouts  22.2 us
  transfers between devices with their start and end apart: 13, of which 10 were waited for; matrix products, arithmetic and copies ran while one was open for 10% of the time, Pallas kernels for 0%

commit v1 on v0

--- a/solution.py
+++ b/solution.py
@@ -312,22 +312,25 @@
     )
     ordered = tuple(attn_shards) + (grad_gate, grad_up, grad_down)
     totals = lax.psum(
-        (
-            ordered[0],
-            ordered[1],
-            ordered[2],
-            ordered[3],
-            ordered[4],
-            ordered[5],
-            ordered[6],
-            ordered[7],
-            ordered[8],
-            ordered[9],
-            ordered[10],
-            ordered[11],
-            ordered[12],
+        lax.psum(
+            (
+                ordered[0],
+                ordered[1],
+                ordered[2],
+                ordered[3],
+                ordered[4],
+                ordered[5],
+                ordered[6],
+                ordered[7],
+                ordered[8],
+                ordered[9],
+                ordered[10],
+                ordered[11],
+                ordered[12],
+            ),
+            "ctx",
         ),
-        ("seq", "ctx"),
+        "seq",
     )
     result = result.reshape(seq_count, seq_rows, model_width)
     input_grad = input_grad.reshape(seq_count, seq_rows, model_width)

time: 595 us -> 687 us (1.15)
  waiting for transfers between devices: 247 us -> 340 us
    psum x1, waiting for transfers between devices: 20.6 us -> 80.2 us  [on_device(): lax.psum((ordered[0], ordered[1], ordered[2], ordered[3], ordered[4], ord...]
    psum x0 -> x1, waiting for transfers between devices: none -> 29.7 us  [on_device(): lax.psum(lax.psum((ordered[0], ordered[1], ordered[2], ordered[3], ordere...]
    psum x1, blocking collectives: 126 us -> 118 us  [on_device(): lax.psum((ordered[0], ordered[1], ordered[2], ordered[3], ordered[4], ord...]
    unnamed x217 -> x223, local copies, waits for them, and re-layouts: 22.2 us -> 27 us
    unnamed x15 -> x16, waiting for transfers between devices: 53.9 us -> 53.9 us
  transfers between devices with their start and end apart: 13 -> 14, of which waited for: 10 -> 11; matrix products, arithmetic and copies ran while one was open for 10% -> 9% of each run, Pallas kernels for 0% -> 0%
where the time goes in v1:
time: 687 us; the launch traced here: 686 us
  waiting for transfers between devices  340 us (49%)
  blocking collectives  207 us (30%)
  matrix products  54.7 us (8%)
  local copies, waits for them, and re-layouts  33.5 us (5%)
  other arithmetic  31.3 us (5%)
  between operations  18.7 us (3%)
    psum x1, blocking collectives, on_device(): lax.psum((ordered[0], ordered[1], ordered[2], ordered[3], ordered[4], ord...  118 us
    psum x1, waiting for transfers between devices, on_device(): lax.psum((ordered[0], ordered[1], ordered[2], ordered[3], ordered[4], ord...  80.2 us
    unnamed x16, waiting for transfers between devices  53.9 us
    unnamed x3, blocking collectives  34.3 us
    reduce_scatter x1, waiting for transfers between devices, on_device(): lax.psum_scatter(grad_out_w.astype(jnp.bfloat16), 'fsdp', scatter_dimensi...  32.8 us
    reduce_scatter x1, waiting for transfers between devices, on_device(): lax.psum_scatter(grad_query_w.astype(jnp.bfloat16), 'fsdp', scatter_dimen...  32.7 us
    psum x1, waiting for transfers between devices, on_device(): lax.psum(lax.psum((ordered[0], ordered[1], ordered[2], ordered[3], ordere...  29.7 us
    all_gather x1, waiting for transfers between devices, on_device(): lax.all_gather(ffn_grad.reshape(seq_count, seq_rows, model_width), 'fsdp'...  28.9 us
  transfers between devices with their start and end apart: 14, of which 11 were waited for; matrix products, arithmetic and copies ran while one was open for 9% of the time, Pallas kernels for 0%

profile of v1, /device:TPU:0, one launch (start us, length us, event | category | flops | bytes accessed | tf_op | source)
XLA Modules:
  0.0 685.9 jit_solution(7208193545013486004)
XLA Ops:
  16.1 13.4 %all-reduce = bf16[8]{0:T(256)(128)(2,1)S(1)} all-reduce(bf16[8]{0:T(256)(128)(2,1)S(1)} %dynamic-update-slice), channel_id=1, replica_groups=mesh['seq'=2,'ctx'=4,'fsdp'=4] {'ctx'}, use_global_device_ids=true, to_apply=%add | all-reduce | flops 8 | bytes 32
  34.7 10.8 %all-reduce.20 = (bf16[640]{0:T(1024)(128)(2,1)S(1)}, bf16[256]{0:T(256)(128)(2,1)S(1)}, bf16[256]{0:T(256)(128)(2,1)S(1)}, bf16[640]{0:T(1024)(128)(2,1)S(1)}, ...) all-reduce(bf16[640]{0:T(1024)(128)(2,1)S(1)} %dynamic-update-slice, ...), channel_id=1, replica_groups=mesh['seq'=2,'ctx'=4,'fsdp'=4] {'fsdp'}, use_global_device_ids=true, to_apply=%add.1 | all-reduce | flops 3072 | bytes 12288
  45.6 9.6 %all_gather.49 = bf16[640,256]{1,0:T(8,128)(2,1)S(1)} all-gather(bf16[160,256]{1,0:T(8,128)(2,1)} %param.21), channel_id=1, replica_groups=mesh['seq'=2,'ctx'=4,'fsdp'=4] {'fsdp'}, dimensions={0}, use_global_device_ids=true | all-gather | bytes 409600 | tf_op jit(solution)/shard_map/all_gather | solution.py:119
  55.2 1.5 multiply_reduce_fusion.13
  56.8 11.6 %all_gather.52 = bf16[640,256]{1,0:T(8,128)(2,1)S(1)} all-gather(bf16[160,256]{1,0:T(8,128)(2,1)S(1)} %copy-done.60), channel_id=1, replica_groups=mesh['seq'=2,'ctx'=4,'fsdp'=4] {'fsdp'}, dimensions={0}, use_global_device_ids=true | all-gather | bytes 409600 | tf_op jit(solution)/shard_map/all_gather | solution.py:120
  68.7 15.6 %all-gather = bf16[1024,256]{1,0:T(8,128)(2,1)} all-gather(bf16[256,256]{1,0:T(8,128)(2,1)S(1)} %convolution_convert_fusion.10), channel_id=2, replica_groups=mesh['seq'=2,'ctx'=4,'fsdp'=4] {'ctx'}, dimensions={0}, use_global_device_ids=true | all-gather | bytes 655360 | tf_op jit(solution)/shard_map/all_gather | solution.py:162
  85.7 14.7 %all_gather.51 = bf16[1,1024,256]{1,2,0:T(8,128)(2,1)S(1)} all-gather(bf16[1,256,256]{1,2,0:T(8,128)(2,1)S(1)} %pad_maximum_fusion.5), channel_id=1, replica_groups=mesh['seq'=2,'ctx'=4,'fsdp'=4] {'ctx'}, dimensions={1}, use_global_device_ids=true | all-gather | bytes 655360 | tf_op jit(solution)/shard_map/all_gather | solution.py:161
  100.4 2.4 copy.46
  102.8 2.0 multiply_reduce_fusion.6
  112.1 2.2 multiply_reduce_fusion.10
  117.1 27.0 %all-gather.13.cloned.1.call-done = bf16[1024,640]{1,0:T(8,128)(2,1)} async-done(((bf16[256,640]{1,0:T(8,128)(2,1)}), bf16[1024,640]{1,0:T(8,128)(2,1)}) %all-gather.13.cloned.1.call-update) | async-done | bytes 1310736 | tf_op jit(solution)/shard_map/all_gather | solution.py:185
  144.1 2.6 fusion.139
  146.7 2.6 multiply_convert_fusion.1
  150.3 2.0 convolution_convert_fusion.2
  153.7 28.2 %reduce-scatter.25.cloned.1.call-done = bf16[1,256,640]{2,1,0:T(8,128)(2,1)} async-done(((bf16[4,256,640]{2,1,0:T(8,128)(2,1)}), bf16[1,256,640]{2,1,0:T(8,128)(2,1)}) %reduce-scatter.25.cloned.1.call-update) | async-done | bytes 327696
  183.0 2.0 fusion.65
  185.0 2.0 fusion.64
  187.1 28.9 %all-gather.11.cloned.1.call-done = bf16[4,256,640]{2,1,0:T(8,128)(2,1)} async-done(((bf16[1,256,640]{2,1,0:T(8,128)(2,1)}), bf16[4,256,640]{2,1,0:T(8,128)(2,1)}) %all-gather.11.cloned.1.call-update) | async-done | bytes 1310736 | tf_op jit(solution)/shard_map/all_gather | solution.py:208
  216.0 5.0 multiply_convert_fusion
  222.7 2.1 add_convert_fusion
  230.0 24.2 %reduce-scatter.27.cloned.1.call-done = bf16[1,256,640]{2,1,0:T(8,128)(2,1)} async-done(((bf16[4,256,640]{2,1,0:T(8,128)(2,1)}), bf16[1,256,640]{2,1,0:T(8,128)(2,1)}) %reduce-scatter.27.cloned.1.call-update) | async-done | bytes 327696
  254.2 2.1 fusion.66
  256.3 3.5 multiply_reduce_fusion.7
  263.2 2.8 fusion.133
  267.8 1.4 multiply_reduce_fusion.4
  270.4 1.3 multiply_reduce_fusion.3
  273.7 2.0 multiply_convert_fusion.6
  282.0 13.5 %reduce-scatter.15.cloned.1.call-done = bf16[1,256,256]{2,1,0:T(8,128)(2,1)} async-done(((bf16[1,1024,256]{2,1,0:T(8,128)(2,1)}), bf16[1,256,256]{2,1,0:T(8,128)(2,1)}) %reduce-scatter.15.cloned.1.call-update) | async-done | bytes 131088 | tf_op jit(solution)/shard_map/reduce_scatter | solution.py:257
  295.4 2.0 convolution_convert_fusion.4
  297.5 20.7 %reduce-scatter.13.cloned.1.call-done = bf16[1,256,256]{1,2,0:T(8,128)(2,1)} async-done(((bf16[1,1024,256]{1,2,0:T(8,128)(2,1)}), bf16[1,256,256]{1,2,0:T(8,128)(2,1)}) %reduce-scatter.13.cloned.1.call-update) | async-done | bytes 131088 | tf_op jit(solution)/shard_map/reduce_scatter | solution.py:254
  321.3 1.6 convolution_convert_fusion
  323.6 1.4 fusion.14
  325.0 1.4 fusion.15
  328.1 1.7 convolution_convert_fusion.1
  329.9 3.9 fusion.144
  333.8 1.9 fusion.143
  335.8 1.9 fusion.142
  340.7 10.1 %all-reduce.19 = (bf16[640]{0:T(1024)(128)(2,1)S(1)}, bf16[256]{0:T(256)(128)(2,1)S(1)}, bf16[256]{0:T(256)(128)(2,1)S(1)}, bf16[640]{0:T(1024)(128)(2,1)S(1)}, ...) all-reduce(bf16[640]{0:T(1024)(128)(2,1)S(1)} %get-tuple-element.21, ...), channel_id=12, replica_groups=mesh['seq'=2,'ctx'=4,'fsdp'=4] {'fsdp'}, use_global_device_ids=true, to_apply=%region_47.48.clone | all-reduce | flops 3072 | bytes 12288
  351.0 20.1 %reduce-scatter.19.cloned.1.call-done = bf16[160,256]{1,0:T(8,128)(2,1)} async-done(((bf16[640,256]{1,0:T(8,128)(2,1)}), bf16[160,256]{1,0:T(8,128)(2,1)}) %reduce-scatter.19.cloned.1.call-update) | async-done | bytes 81936 | tf_op jit(solution)/shard_map/reduce_scatter | solution.py:285
  371.1 32.8 %reduce-scatter.23.cloned.1.call-done = bf16[256,640]{1,0:T(8,128)(2,1)} async-done(((bf16[1024,640]{1,0:T(8,128)(2,1)}), bf16[256,640]{1,0:T(8,128)(2,1)}) %reduce-scatter.23.cloned.1.call-update) | async-done | bytes 327696 | tf_op jit(solution)/shard_map/reduce_scatter | solution.py:291
  404.0 32.7 %reduce-scatter.17.cloned.1.call-done = bf16[160,1024]{1,0:T(8,128)(2,1)} async-done(((bf16[640,1024]{1,0:T(8,128)(2,1)}), bf16[160,1024]{1,0:T(8,128)(2,1)}) %reduce-scatter.17.cloned.1.call-update) | async-done | bytes 327696 | tf_op jit(solution)/shard_map/reduce_scatter | solution.py:282
  436.7 118.1 %all-reduce.28 = (f32[160,1024]{1,0:T(8,128)}, f32[160,256]{1,0:T(8,128)}, f32[160,256]{1,0:T(8,128)}, f32[256,640]{1,0:T(8,128)}, f32[160]{0:T(256)S(1)}, /*ind...) all-reduce(bf16[160,1024]{1,0:T(8,128)(2,1)} %reduce-scatter.17.clo, ...), channel_id=1, replica_groups=mesh['seq'=2,'ctx'=4,'fsdp'=4] {'ctx'}, use_global_device_ids=true, to_apply=%region_29.30 | all-reduce | flops 410368 | bytes 2463744 | tf_op jit(solution)/shard_map/psum | solution.py:315
  554.8 80.2 %all-reduce.25.cloned.1.call-done = (f32[640,512]{1,0:T(8,128)}, f32[640,512]{1,0:T(8,128)}, f32[512,640]{1,0:T(8,128)}) async-done(((f32[640,512]{1,0:T(8,128)}, f32[640,512]{1,0:T(8,128)}, f32[512,640]{1,0:T(8,128)}), (f32[640,512]{1,0:T(8,128)}, f32[640,512]{1,0:T(8,128)}, f32[512,640]{1,0:T(8,128)})) %all-reduce.25.cloned.1.call-update) | async-done | bytes 3932176 | tf_op jit(solution)/shard_map/psum | solution.py:315
  637.1 3.0 all-reduce.17
  640.2 29.7 %all-reduce.27.cloned.1.call-done = (f32[160,1024]{1,0:T(8,128)}, f32[160,256]{1,0:T(8,128)}, f32[160,256]{1,0:T(8,128)}, f32[256,640]{1,0:T(8,128)}, f32[640,51...) async-done(((f32[160,1024]{1,0:T(8,128)}, f32[160,256]{1,0:T(8,128)}, f32[160,256]{1,0:T(8,128)}, f32[256,640]{1,0:T(8,128)}, f32[640,512]{1,0:T(8,128)}, ...) | async-done | bytes 5570576 | tf_op jit(solution)/shard_map/psum | solution.py:314
  669.9 2.1 copy.114
  672.0 1.6 copy.115
  673.6 1.7 copy.116
  (340 shorter events, 61.3 us)
Async XLA Ops:
  7.2 143.2 %copy-start = (bf16[512,640]{1,0:T(8,128)(2,1)S(1)}, bf16[512,640]{1,0:T(8,128)(2,1)}, u32[]{:S(2)}) copy-start(bf16[512,640]{1,0:T(8,128)(2,1)} %param.26) | copy-start | bytes 1966084
  7.2 61.2 %copy-start.12 = (bf16[1,256,640]{2,1,0:T(8,128)(2,1)S(1)}, bf16[1,256,640]{2,1,0:T(8,128)(2,1)}, u32[]{:S(2)}) copy-start(bf16[1,256,640]{2,1,0:T(8,128)(2,1)} %param.17) | copy-start | bytes 983044
  7.2 49.6 %copy-start.60 = (bf16[160,256]{1,0:T(8,128)(2,1)S(1)}, bf16[160,256]{1,0:T(8,128)(2,1)}, u32[]{:S(2)}) copy-start(bf16[160,256]{1,0:T(8,128)(2,1)} %param.22) | copy-start | bytes 245764
  7.2 93.2 %all-gather.7.cloned.1.call-start = ((), (), s32[]{:S(2)}) async-start(), calls=%async_computation.8 | async-start | bytes 1638400 | tf_op jit(solution)/shard_map/all_gather | solution.py:118
  8.0 104.2 %all-gather.9.cloned.1.call-start = ((), (), s32[]{:S(2)}) async-start(), calls=%async_computation.9 | async-start | bytes 1638400 | tf_op jit(solution)/shard_map/all_gather | solution.py:121
  8.7 135.4 %all-gather.13.cloned.1.call-start = ((), (), s32[]{:S(2)}) async-start(), calls=%async_computation.17 | async-start | bytes 1638400 | tf_op jit(solution)/shard_map/all_gather | solution.py:185
  8.8 75.7 %copy-start.92 = (f32[128]{0:T(128)}, f32[128]{0:T(128)S(1)}, u32[]{:S(2)}) copy-start(f32[128]{0:T(128)S(1)} %negate_power_fusion) | copy-start | bytes 1540
  13.8 89.0 %copy-start.61 = (f32[256]{0:T(256)}, f32[256]{0:T(256)S(1)}, u32[]{:S(2)}) copy-start(f32[256]{0:T(256)S(1)} %add_rsqrt_fusion.5) | copy-start | bytes 3076
  16.1 69.6 %copy-start.77 = (f32[1,256]{1,0:T(1,128)}, f32[1,256]{1,0:T(1,128)S(1)}, u32[]{:S(2)}) copy-start(f32[1,256]{1,0:T(1,128)S(1)} %convert_element_type.233) | copy-start | bytes 3076
  29.7 76.0 %copy-start.94 = (s32[256]{0:T(256)}, s32[256]{0:T(256)S(1)}, u32[]{:S(2)}) copy-start(s32[256]{0:T(256)S(1)} %bitcast_add_fusion.1) | copy-start | bytes 3076
  45.5 59.4 %copy-start.73 = (f32[256]{0:T(256)}, f32[256]{0:T(256)S(1)}, u32[]{:S(2)}) copy-start(f32[256]{0:T(256)S(1)} %convert_element_type.232) | copy-start | bytes 3076
  45.5 38.9 %copy-start.75 = (f32[256]{0:T(256)}, f32[256]{0:T(256)S(1)}, u32[]{:S(2)}) copy-start(f32[256]{0:T(256)S(1)} %convert_element_type.236) | copy-start | bytes 3076
  45.6 60.1 %copy-start.82 = (s32[1024]{0:T(1024)}, s32[1024]{0:T(1024)S(1)}, u32[]{:S(2)}) copy-start(s32[1024]{0:T(1024)S(1)} %bitcast_add_fusion) | copy-start | bytes 12292
  55.2 30.4 %copy-start.40 = (bf16[640,256]{1,0:T(8,128)(2,1)}, bf16[640,256]{1,0:T(8,128)(2,1)S(1)}, u32[]{:S(2)}) copy-start(bf16[640,256]{1,0:T(8,128)(2,1)S(1)} %all_gather.49) | copy-start | bytes 983044
  56.8 28.9 %copy-start.35 = (f32[256,256]{0,1:T(8,128)}, f32[256,256]{0,1:T(8,128)S(1)}, u32[]{:S(2)}) copy-start(f32[256,256]{0,1:T(8,128)S(1)} %get-tuple-element.95) | copy-start | bytes 786436
  56.8 27.7 %copy-start.67 = (f32[256]{0:T(256)}, f32[256]{0:T(256)S(1)}, u32[]{:S(2)}) copy-start(f32[256]{0:T(256)S(1)} %add_rsqrt_fusion.4) | copy-start | bytes 3076
  68.4 17.3 %copy-start.42 = (bf16[640,256]{1,0:T(8,128)(2,1)}, bf16[640,256]{1,0:T(8,128)(2,1)S(1)}, u32[]{:S(2)}) copy-start(bf16[640,256]{1,0:T(8,128)(2,1)S(1)} %all_gather.52) | copy-start | bytes 983044
  85.7 19.4 %copy-start.44 = (f32[256,128]{0,1:T(8,128)}, f32[256,128]{0,1:T(8,128)S(1)}, u32[]{:S(2)}) copy-start(f32[256,128]{0,1:T(8,128)S(1)} %get-tuple-element.87) | copy-start | bytes 393220
  105.7 4.0 copy-start.5
  106.1 4.1 copy-start.2
  106.1 4.1 copy-start.85
  116.9 65.0 %reduce-scatter.25.cloned.1.call-start = ((), (), s32[]{:S(2)}) async-start(), calls=%async_computation.18 | async-start | bytes 1638400
  152.4 63.6 %all-gather.11.cloned.1.call-start = ((), (), s32[]{:S(2)}) async-start(), calls=%async_computation.10 | async-start | bytes 1638400 | tf_op jit(solution)/shard_map/all_gather | solution.py:208
  187.1 67.2 %reduce-scatter.27.cloned.1.call-start = ((), (), s32[]{:S(2)}) async-start(), calls=%async_computation.19 | async-start | bytes 1638400
  216.0 5.1 copy-start.53
  224.7 31.6 %copy-start.16 = (f32[256,640]{1,0:T(8,128)S(1)}, f32[256,640]{1,0:T(8,128)}, u32[]{:S(2)}) copy-start(f32[256,640]{1,0:T(8,128)} %copy-done.15) | copy-start | bytes 1966084
  224.8 70.7 %reduce-scatter.15.cloned.1.call-start = ((), (), s32[]{:S(2)}) async-start(), calls=%async_computation.12 | async-start | bytes 655360 | tf_op jit(solution)/shard_map/reduce_scatter | solution.py:257
  254.2 5.6 copy-start.70
  256.3 5.1 copy-start.23
  265.9 6.2 copy-start.50
  273.7 44.5 %reduce-scatter.13.cloned.1.call-start = ((), (), s32[]{:S(2)}) async-start(), calls=%async_computation.11 | async-start | bytes 655360 | tf_op jit(solution)/shard_map/reduce_scatter | solution.py:254
  279.6 15.8 %copy-start.14 = (bf16[1,256,640]{2,1,0:T(8,128)(2,1)S(1)}, bf16[1,256,640]{2,1,0:T(8,128)(2,1)}, u32[]{:S(2)}) copy-start(bf16[1,256,640]{2,1,0:T(8,128)(2,1)} %param.17) | copy-start | bytes 983044
  279.6 15.8 %copy-start.62 = (f32[256]{0:T(256)S(1)}, f32[256]{0:T(256)}, u32[]{:S(2)}) copy-start(f32[256]{0:T(256)} %copy-done.61) | copy-start | bytes 3076
  280.7 38.4 %copy-start.78 = (f32[1,256]{1,0:T(1,128)S(1)}, f32[1,256]{1,0:T(1,128)}, u32[]{:S(2)}) copy-start(f32[1,256]{1,0:T(1,128)} %copy-done.77) | copy-start | bytes 3076
  280.7 38.4 %copy-start.93 = (f32[128]{0:T(128)S(1)}, f32[128]{0:T(128)}, u32[]{:S(2)}) copy-start(f32[128]{0:T(128)} %copy-done.92) | copy-start | bytes 1540
  280.7 39.0 %copy-start.36 = (f32[256,256]{0,1:T(8,128)S(1)}, f32[256,256]{0,1:T(8,128)}, u32[]{:S(2)}) copy-start(f32[256,256]{0,1:T(8,128)} %copy-done.35) | copy-start | bytes 786436
  280.7 39.0 %copy-start.68 = (f32[256]{0:T(256)S(1)}, f32[256]{0:T(256)}, u32[]{:S(2)}) copy-start(f32[256]{0:T(256)} %copy-done.67) | copy-start | bytes 3076
  280.7 39.0 %copy-start.76 = (f32[256]{0:T(256)S(1)}, f32[256]{0:T(256)}, u32[]{:S(2)}) copy-start(f32[256]{0:T(256)} %copy-done.75) | copy-start | bytes 3076
  281.9 39.4 %copy-start.26 = (bf16[256,4,256]{0,2,1:T(8,128)(2,1)S(1)}, bf16[256,4,256]{0,2,1:T(8,128)(2,1)}, u32[]{:S(2)}) copy-start(bf16[256,4,256]{0,2,1:T(8,128)(2,1)} %pad_maximum_fusion.2) | copy-start | bytes 1572868
  281.9 39.4 %copy-start.34 = (bf16[256,640]{1,0:T(8,128)(2,1)S(1)}, bf16[256,640]{1,0:T(8,128)(2,1)}, u32[]{:S(2)}) copy-start(bf16[256,640]{1,0:T(8,128)(2,1)} %copy-done.33) | copy-start | bytes 983044
  281.9 69.1 %reduce-scatter.21.cloned.1.call-start = ((), (), s32[]{:S(2)}) async-start(), calls=%async_computation.15 | async-start | bytes 409600 | tf_op jit(solution)/shard_map/reduce_scatter | solution.py:288
  297.5 73.7 %reduce-scatter.19.cloned.1.call-start = ((), (), s32[]{:S(2)}) async-start(), calls=%async_computation.14 | async-start | bytes 409600 | tf_op jit(solution)/shard_map/reduce_scatter | solution.py:285
  321.2 82.8 %reduce-scatter.23.cloned.1.call-start = ((), (), s32[]{:S(2)}) async-start(), calls=%async_computation.16 | async-start | bytes 1638400 | tf_op jit(solution)/shard_map/reduce_scatter | solution.py:291
  322.9 113.7 %reduce-scatter.17.cloned.1.call-start = ((), (), s32[]{:S(2)}) async-start(), calls=%async_computation.13 | async-start | bytes 1638400 | tf_op jit(solution)/shard_map/reduce_scatter | solution.py:282
  329.8 305.2 %all-reduce.25.cloned.1.call-start = ((), (), s32[]{:S(2)}) async-start(), calls=%async_computation.20 | async-start | bytes 7864320 | tf_op jit(solution)/shard_map/psum | solution.py:315
  337.7 332.2 %all-reduce.27.cloned.1.call-start = ((), (), s32[]{:S(2)}) async-start(), calls=%async_computation.21 | async-start | bytes 11141120 | tf_op jit(solution)/shard_map/psum | solution.py:314
  669.9 5.4 copy-start.52
  669.9 6.3 copy-start.39
  (66 other events, 120.7 us)
Sparse Core Ops, SparseCore 0:
  9.9 32.2 all-gather.6
  44.0 29.9 all-gather.8
  117.0 27.0 all-gather.12
  152.5 29.3 reduce-scatter.24
  187.2 28.7 all-gather.10
  224.9 29.2 reduce-scatter.26
  273.8 21.6 reduce-scatter.14
  298.3 19.8 reduce-scatter.12
  321.0 22.5 reduce-scatter.20
  346.8 24.2 reduce-scatter.18
  374.6 29.2 reduce-scatter.22
  407.3 29.2 reduce-scatter.16
  439.8 195.1 all-reduce.24
  639.3 30.5 all-reduce.26
